TPU v7x, 32 devices: a whole 2x2x4 slice. The times are simulated.
32 devices in a mesh: dp: 16 (over z, y, core), rep: 2 (over x).
Axes of the slice: x: 2, y: 2, z: 4, core: 2. Of those that a mesh axis runs over, the one named last changes fastest.
Arguments:
- inputs: bfloat16 [32, 256, 768], P(('dp', 'rep')), may hold values from -6 to 6
- norm_gain: float32 [768], replicated, may hold values from 0.5 to 1.5
- in_weight: bfloat16 [768, 3352], P('dp'), may hold values from -0.21875 to 0.21875
- conv_weight: float32 [4, 1792], replicated, may hold values from -3 to 3
- conv_bias: float32 [1792], replicated, may hold values from -3 to 3
- dt_bias: float32 [24], replicated, may hold values from -6 to -1
- a_log: float32 [24], replicated, may hold values from -2 to 1.5
- skip_gain: float32 [24], replicated, may hold values from 0.5 to 2
- gate_gain: float32 [1536], replicated, may hold values from 0.5 to 1.5
- out_weight: bfloat16 [1536, 768], P('dp'), may hold values from -0.15625 to 0.15625
- cotangent: bfloat16 [32, 256, 768], P(('dp', 'rep')), may hold values from -6 to 6
Outputs:
- output: bfloat16 [32, 256, 768], P(('dp', 'rep'))
- grad_inputs: bfloat16 [32, 256, 768], P(('dp', 'rep'))
- grad_norm_gain: float32 [768], replicated
- grad_in_weight: float32 [768, 3352], P('dp')
- grad_conv_weight: float32 [4, 1792], replicated
- grad_conv_bias: float32 [1792], replicated
- grad_dt_bias: float32 [24], replicated
- grad_a_log: float32 [24], replicated
- grad_skip_gain: float32 [24], replicated
- grad_gate_gain: float32 [1536], replicated
- grad_out_weight: float32 [1536, 768], P('dp')
All inputs are finite; a program needn't handle non-finite values.
Results may differ from a plain program's by a relative error of at most 0.0082.
Values may be sent and summed in bfloat16 or wider, within the bound.
A program may use at most 128 MiB of HBM per device.

v0:
```python
import jax
import jax.numpy as jnp
from jax import lax
from jax.sharding import PartitionSpec as P

SPAN = 256


def head_mix(values, step_size, decay_rate, b_blocks, c_blocks, scores):
    length = values.shape[1]
    scaled = step_size * decay_rate
    running = jnp.cumsum(scaled, axis=1)
    row_ids = lax.broadcasted_iota(jnp.int32, (length, length), 0)
    col_ids = lax.broadcasted_iota(jnp.int32, (length, length), 1)
    causal = row_ids >= col_ids
    spread = running[:, :, None] - running[:, None, :]
    decays = jnp.exp(jnp.where(causal[None], spread, -jnp.inf))
    weight = scores * decays * step_size[:, None, :]
    within = jnp.einsum("cqs,csp->cqp", weight, values, precision=lax.Precision.HIGHEST)
    to_end = jnp.exp(running[:, -1:] - running) * step_size
    states = jnp.einsum(
        "cs,csn,csp->cnp", to_end, b_blocks, values, precision=lax.Precision.HIGHEST
    )
    before = jnp.zeros(states.shape[1:], states.dtype)
    priors = [before]
    carried = jnp.stack(priors)
    across = jnp.einsum("cqn,cnp->cqp", c_blocks, carried, precision=lax.Precision.HIGHEST)
    return within + across * jnp.exp(running)[:, :, None]


def mixer(projected, conv_weight, conv_bias, dt_bias, a_log, skip_gain, gate_gain):
    length = projected.shape[0]
    inner_width = gate_gain.shape[0]
    head_count = skip_gain.shape[0]
    channels = conv_bias.shape[0]
    state_width = (channels - inner_width) // 2
    tap_count = conv_weight.shape[0]
    gate_in = projected[:, :inner_width]
    conv_in = projected[:, inner_width : inner_width + channels]
    step_raw = projected[:, inner_width + channels :]
    padded = jnp.pad(conv_in, ((tap_count - 1, 0), (0, 0)))
    convolved = conv_bias + jnp.zeros_like(conv_in)
    for offset in range(tap_count):
        convolved = convolved + conv_weight[offset] * padded[offset : offset + length]
    active = jax.nn.silu(convolved)
    values = active[:, :inner_width]
    b_proj = active[:, inner_width : inner_width + state_width]
    c_proj = active[:, inner_width + state_width :]
    step_size = jax.nn.softplus(step_raw + dt_bias)
    decay_rate = -jnp.exp(a_log)
    blocks = length // SPAN
    b_blocks = b_proj.reshape(blocks, SPAN, state_width)
    c_blocks = c_proj.reshape(blocks, SPAN, state_width)
    scores = jnp.einsum("cqn,csn->cqs", c_blocks, b_blocks, precision=lax.Precision.HIGHEST)
    head_values = values.reshape(blocks, SPAN, head_count, inner_width // head_count).transpose(
        2, 0, 1, 3
    )
    head_steps = step_size.reshape(blocks, SPAN, head_count).transpose(2, 0, 1)

    def one_head(member):
        return head_mix(member[0], member[1], member[2], b_blocks, c_blocks, scores)

    mixed_heads = lax.map(jax.checkpoint(one_head), (head_values, head_steps, decay_rate))
    scanned = mixed_heads.transpose(1, 2, 0, 3).reshape(length, inner_width)
    skipped = values.reshape(length, head_count, inner_width // head_count) * skip_gain[:, None]
    scanned = scanned + skipped.reshape(length, inner_width)
    gated_out = scanned * jax.nn.silu(gate_in)
    return (
        gated_out
        * lax.rsqrt(jnp.mean(gated_out * gated_out, axis=-1, keepdims=True) + 1e-05)
        * gate_gain
    )


def front_norm(rows_in, norm_gain):
    return (
        rows_in * lax.rsqrt(jnp.mean(rows_in * rows_in, axis=-1, keepdims=True) + 1e-05) * norm_gain
    )


def local(
    inputs,
    norm_gain,
    in_weight,
    conv_weight,
    conv_bias,
    dt_bias,
    a_log,
    skip_gain,
    gate_gain,
    out_weight,
    cotangent,
):
    in_full, out_full = (
        lax.all_gather(in_weight, "dp", axis=0, tiled=True),
        lax.all_gather(out_weight, "dp", axis=0, tiled=True),
    )
    seq_count, length, model_width = inputs.shape
    total_rows = seq_count * length
    rows_in = inputs.astype(jnp.float32).reshape(total_rows, model_width)
    normed, norm_back = jax.vjp(front_norm, rows_in, norm_gain)
    normed_low = normed.astype(jnp.bfloat16)
    projected = jnp.dot(normed_low, in_full, preferred_element_type=jnp.float32)
    projected = projected.reshape(seq_count, length, projected.shape[-1])
    mix_all = jax.vmap(mixer, in_axes=(0, None, None, None, None, None, None))
    mixed, mix_back = jax.vjp(
        mix_all, projected, conv_weight, conv_bias, dt_bias, a_log, skip_gain, gate_gain
    )
    mixed_low = mixed.reshape(total_rows, mixed.shape[-1]).astype(jnp.bfloat16)
    result = rows_in + jnp.dot(mixed_low, out_full, preferred_element_type=jnp.float32)
    output = result.astype(jnp.bfloat16).reshape(inputs.shape)
    in_back, out_back = (
        lax.all_gather(in_weight, "dp", axis=0, tiled=True),
        lax.all_gather(out_weight, "dp", axis=0, tiled=True),
    )
    cotangent_rows = cotangent.reshape(total_rows, model_width)
    grad_out_w = jnp.einsum(
        "rk,rd->kd", mixed_low, cotangent_rows, preferred_element_type=jnp.float32
    )
    grad_mixed = jnp.einsum(
        "rd,kd->rk", cotangent_rows, out_back, preferred_element_type=jnp.float32
    )
    mix_grads = mix_back(grad_mixed.reshape(mixed.shape))
    grad_proj_low = mix_grads[0].reshape(total_rows, projected.shape[-1]).astype(jnp.bfloat16)
    grad_in_w = jnp.einsum(
        "rd,rp->dp", normed_low, grad_proj_low, preferred_element_type=jnp.float32
    )
    grad_normed = jnp.einsum(
        "rp,dp->rd", grad_proj_low, in_back, preferred_element_type=jnp.float32
    )
    grad_rows, grad_norm = norm_back(grad_normed)
    grad_inputs = (
        (cotangent_rows.astype(jnp.float32) + grad_rows).astype(jnp.bfloat16).reshape(inputs.shape)
    )
    half_in, half_out = (
        lax.psum_scatter(grad_in_w, ("dp", "rep"), scatter_dimension=0, tiled=True),
        lax.psum_scatter(grad_out_w, ("dp", "rep"), scatter_dimension=0, tiled=True),
    )
    owned_in, owned_out = (
        lax.all_gather(half_in.astype(jnp.bfloat16), "rep", axis=0, tiled=True).astype(
            half_in.dtype
        ),
        lax.all_gather(half_out.astype(jnp.bfloat16), "rep", axis=0, tiled=True).astype(
            half_out.dtype
        ),
    )
    summed = lax.psum(
        (
            grad_norm,
            mix_grads[1],
            mix_grads[2],
            mix_grads[3],
            mix_grads[4],
            mix_grads[5],
            mix_grads[6],
        ),
        ("dp", "rep"),
    )
    return (
        output,
        grad_inputs,
        summed[0],
        owned_in,
        summed[1],
        summed[2],
        summed[3],
        summed[4],
        summed[5],
        summed[6],
        owned_out,
    )


def solution(mesh):
    placed = (
        P(("dp", "rep"), None, None),
        P(),
        P("dp", None),
        P(),
        P(),
        P(),
        P(),
        P(),
        P(),
        P("dp", None),
        P(("dp", "rep"), None, None),
    )
    return jax.shard_map(
        local,
        mesh=mesh,
        in_specs=placed,
        out_specs=(
            P(("dp", "rep"), None, None),
            P(("dp", "rep"), None, None),
            P(),
            P("dp", None),
            P(),
            P(),
            P(),
            P(),
            P(),
            P(),
            P("dp", None),
        ),
        check_vma=False,
    )
```

profile of v0, /device:TPU:0, one launch (start us, length us, event | category | flops | bytes accessed | tf_op | source)
XLA Modules:
  0.0 713.6 jit_solution(2319859396425935077)
XLA Ops:
  12.4 56.8 %all-gather.3.cloned.1.call-done = bf16[768,3352]{1,0:T(8,128)(2,1)} async-done(((bf16[48,3352]{1,0:T(8,128)(2,1)}), bf16[768,3352]{1,0:T(8,128)(2,1)}) %all-gather.3.cloned.1.call-update) | async-done | bytes 5148688 | tf_op jit(solution)/shard_map/all_gather | solution.py:95
  69.2 5.0 convolution_bitcast_fusion.3
  74.9 4.0 fusion.50
  80.5 2.3 copy.55
  83.0 83.4 %while.35 = (s32[]{:T(128)}, f32[24,1,1,256,64]{3,4,2,1,0:T(8,128)S(1)}, f32[24,1,1,256]{3,2,1,0:T(1,128)S(1)}, f32[24]{0:T(128)S(1)}, f32[1,1,256,256]{3,2,1,0:...) while((s32[]{:T(128)}, ...), condition=%wide.region_4.5_spmd.clone, body=%wide.region_1.4_spmd.clone.sunk | while | flops 50725124 | bytes 539837 | solution.py:63
  167.6 2.5 multiply_reduce_fusion.6
  171.2 3.0 fusion.82
  174.2 4.3 fusion.54
  180.5 4.9 multiply_reduce_fusion.5
  186.7 347.8 %while.36 = (s32[]{:T(128)}, f32[1,1,256,256]{3,2,1,0:T(8,128)}, f32[1,1,256,128]{3,2,1,0:T(8,128)}, f32[24,1,1,256,64]{3,4,2,1,0:T(8,128)}, f32[24,1,1,256]{3,0...) while((s32[]{:T(128)}, f32[1,1,256,256]{3,2,1,0:T(8,128)}, ...), condition=%wide.region_17.18_spmd.clone, body=%wide.region_7.17_spmd.clone.sunk | while | flops 152684288 | bytes 3709364 | solution.py:63
  191.9 2.3 fusion.149
  205.4 2.4 fusion.149
  207.8 2.0 fusion.150
  220.0 2.4 fusion.149
  222.3 2.0 fusion.150
  234.5 2.3 fusion.149
  236.9 2.0 fusion.150
  249.1 2.3 fusion.149
  263.6 2.4 fusion.149
  265.9 2.0 fusion.150
  278.1 2.4 fusion.149
  280.5 2.0 fusion.150
  292.6 2.3 fusion.149
  307.2 2.3 fusion.149
  321.7 2.3 fusion.149
  336.2 2.3 fusion.149
  350.8 2.3 fusion.149
  365.3 2.3 fusion.149
  379.8 2.3 fusion.149
  394.3 2.3 fusion.149
  408.9 2.3 fusion.149
  423.4 2.3 fusion.149
  437.9 2.3 fusion.149
  452.4 2.3 fusion.149
  467.0 2.3 fusion.149
  481.5 2.3 fusion.149
  496.0 2.3 fusion.149
  510.5 2.3 fusion.149
  525.1 2.3 fusion.149
  540.4 2.3 multiply_add_fusion.1
  543.3 4.6 multiply_reduce_fusion.3
  552.3 5.8 fusion.79
  559.1 5.5 fusion.68
  564.7 40.6 %all-reduce.16 = (f32[768]{0:T(1024)}, f32[4,1792]{1,0:T(4,128)}, f32[1792]{0:T(1024)}, f32[24]{0:T(128)}, f32[24]{0:T(128)}, /*index=5*/f32[24]{0:T(128)}, f32[1536]{0:T(1024)}) all-reduce(f32[768]{0:T(1024)S(1)} %get-tuple-element.481, f32[4,1792]{1,0:T(4,128)S(1)} %pad_add_fusion.3, ...), channel_id=1, replica_groups=mesh['dp'=16,'rep'=2] {'dp','rep'}, use_global_device_ids=true, to_apply=%region_20.21 | all-reduce | flops 11336 | bytes 90688 | tf_op jit(solution)/shard_map/psum | solution.py:147
  606.3 3.4 fusion.58
  610.7 6.9 all_gather.17
  618.3 80.9 %reduce-scatter.7.cloned.1.call-done = f32[24,3352]{1,0:T(8,128)} async-done(((f32[768,3352]{1,0:T(8,128)}), f32[24,3352]{1,0:T(8,128)}) %reduce-scatter.7.cloned.1.call-update) | async-done | bytes 321808
  700.2 6.0 all_gather.16
  (1017 shorter events, 393.0 us)
Async XLA Ops:
  7.2 62.1 %all-gather.3.cloned.1.call-start = ((), (), s32[]{:S(2)}) async-start(), calls=%async_computation.2 | async-start | bytes 5640192 | tf_op jit(solution)/shard_map/all_gather | solution.py:95
  7.9 166.3 %all-gather.5.cloned.1.call-start = ((), (), s32[]{:S(2)}) async-start(), calls=%async_computation.3 | async-start | bytes 2506752 | tf_op jit(solution)/shard_map/all_gather | solution.py:96
  8.7 601.1 %reduce-scatter.5.cloned.1.call-start = ((), (), s32[]{:S(2)}) async-start(), calls=%async_computation.4 | async-start | bytes 4866048 | tf_op jit(solution)/shard_map/reduce_scatter | solution.py:137
  9.9 64.3 %copy-start.29 = (f32[256]{0:T(256)}, f32[256]{0:T(256)S(1)}, u32[]{:S(2)}) copy-start(f32[256]{0:T(256)S(1)} %fusion.104) | copy-start | bytes 3076
  11.6 62.8 %copy-start.15 = (f32[1792]{0:T(1024)}, f32[1792]{0:T(1024)S(1)}, u32[]{:S(2)}) copy-start(f32[1792]{0:T(1024)S(1)} %get-tuple-element.483) | copy-start | bytes 21508
  11.6 62.8 %copy-start.17 = (f32[1792]{0:T(1024)}, f32[1792]{0:T(1024)S(1)}, u32[]{:S(2)}) copy-start(f32[1792]{0:T(1024)S(1)} %get-tuple-element.484) | copy-start | bytes 21508
  11.6 62.8 %copy-start.19 = (f32[1792]{0:T(1024)}, f32[1792]{0:T(1024)S(1)}, u32[]{:S(2)}) copy-start(f32[1792]{0:T(1024)S(1)} %get-tuple-element.485) | copy-start | bytes 21508
  11.6 62.8 %copy-start.21 = (f32[1792]{0:T(1024)}, f32[1792]{0:T(1024)S(1)}, u32[]{:S(2)}) copy-start(f32[1792]{0:T(1024)S(1)} %get-tuple-element.486) | copy-start | bytes 21508
  74.2 6.2 copy-start
  74.4 4.6 copy-start.2
  179.9 519.4 %reduce-scatter.7.cloned.1.call-start = ((), (), s32[]{:S(2)}) async-start(), calls=%async_computation.5 | async-start | bytes 10948608
  180.5 6.2 copy-start.40
  191.8 4.3 copy-start.8
  205.4 4.3 copy-start.11
  205.4 5.3 copy-start.8
  220.0 5.3 copy-start.8
  234.5 5.3 copy-start.8
  249.0 5.3 copy-start.8
  263.6 4.3 copy-start.11
  263.6 5.3 copy-start.8
  278.1 4.3 copy-start.11
  278.1 5.3 copy-start.8
  292.6 5.3 copy-start.8
  307.2 5.3 copy-start.8
  321.7 5.3 copy-start.8
  336.2 5.3 copy-start.8
  350.8 5.3 copy-start.8
  365.3 5.3 copy-start.8
  379.8 5.3 copy-start.8
  394.3 5.3 copy-start.8
  408.9 5.3 copy-start.8
  423.4 5.3 copy-start.8
  437.9 5.3 copy-start.8
  452.4 5.3 copy-start.8
  466.9 5.3 copy-start.8
  481.5 5.3 copy-start.8
  496.0 5.3 copy-start.8
  510.5 5.3 copy-start.8
  525.0 5.3 copy-start.8
  537.9 4.8 copy-start.3
  543.3 4.6 copy-start.16
  543.3 4.6 copy-start.18
  543.3 4.6 copy-start.20
  543.3 4.6 copy-start.22
  559.1 5.6 copy-start.27
  559.1 46.1 %copy-start.32 = (f32[256]{0:T(256)S(1)}, f32[256]{0:T(256)}, u32[]{:S(2)}) copy-start(f32[256]{0:T(256)} %copy-done.31) | copy-start | bytes 3076
  559.1 46.2 %copy-start.10 = (bf16[1,256,768]{2,1,0:T(8,128)(2,1)S(1)}, bf16[1,256,768]{2,1,0:T(8,128)(2,1)}, u32[]{:S(2)}) copy-start(bf16[1,256,768]{2,1,0:T(8,128)(2,1)} %param.25) | copy-start | bytes 1179652
  564.7 41.6 %copy-start.26 = (f32[256]{0:T(256)S(1)}, f32[256]{0:T(256)}, u32[]{:S(2)}) copy-start(f32[256]{0:T(256)} %copy-done.24) | copy-start | bytes 3076
  (45 other events, 132.9 us)
Sparse Core Ops, SparseCore 0:
  10.2 59.0 all-gather.2
  71.5 41.0 all-gather.4
  180.0 106.3 reduce-scatter.4
  558.3 140.8 reduce-scatter.6
where the time goes:
time: 719 us; the launch traced here: 714 us
  matrix products  198 us (28%)
  local copies, waits for them, and re-layouts  155 us (22%)
  other arithmetic  151 us (21%)
  waiting for transfers between devices  139 us (19%)
  blocking collectives  53.5 us (7%)
  between operations  14.3 us (2%)
    dot_general x72, matrix products, head_mix(): jnp.einsum('cqs,csp->cqp', weight, values, precision=lax.Precision.HIGHEST)  115 us
    unnamed x5, waiting for transfers between devices  82.3 us
    squeeze x72, local copies, waits for them, and re-layouts, mixer(): lax.map(jax.checkpoint(one_head), (head_values, head_steps, decay_rate))  74.2 us
    another operation x144, other arithmetic  58 us
    all_gather x1, waiting for transfers between devices, local(): lax.all_gather(in_weight, 'dp', axis=0, tiled=True)  56.8 us
    dot_general x49, matrix products, head_mix(): jnp.einsum('cqn,cnp->cqp', c_blocks, carried, precision=lax.Precision.HIG...  52.9 us
    psum x1, blocking collectives, local(): lax.psum((grad_norm, mix_grads[1], mix_grads[2], mix_grads[3], mix_grads[...  40.6 us
    mul x48, other arithmetic, head_mix(): scaled = step_size * decay_rate  31.2 us
  transfers between devices with their start and end apart: 4, of which 2 were waited for; matrix products, arithmetic and copies ran while one was open for 69% of the time, Pallas kernels for 0%

commit v1 on v0

v1 whole, which is shorter than its diff:
```python
import jax
import jax.numpy as jnp
from jax import lax
from jax.experimental import pallas as pl
from jax.experimental.pallas import tpu as pltpu
from jax.sharding import PartitionSpec as P

EPS = 1e-05
LOW = jnp.bfloat16
F32 = jnp.float32
EXACT = lax.Precision.HIGHEST
PAIR = 2


def dot(a, b, dims, precision=None):
    return lax.dot_general(
        a, b, (dims, ((), ())), precision=precision, preferred_element_type=F32
    )


def spread_of(run_col, run_row, length):
    row_ids = lax.broadcasted_iota(jnp.int32, (length, length), 0)
    col_ids = lax.broadcasted_iota(jnp.int32, (length, length), 1)
    return jnp.exp(jnp.where(row_ids >= col_ids, run_col - run_row, -jnp.inf))


def forward_kernel(values, b_ref, c_ref, run_col, run_row, step_row, out, scores):
    length = values.shape[0]
    width = values.shape[1] // PAIR

    @pl.when(pl.program_id(0) == 0)
    def _():
        scores[...] = dot(c_ref[...], b_ref[...], ((1,), (1,)), EXACT)

    parts = []
    for i in range(PAIR):
        decays = spread_of(run_col[0, :, i : i + 1], run_row[0, i : i + 1, :], length)
        weight = scores[...] * (decays * step_row[0, i : i + 1, :])
        vals = values[:, i * width : (i + 1) * width]
        parts.append(dot(weight.astype(LOW), vals.astype(LOW), ((1,), (0,))))
    out[...] = jnp.concatenate(parts, axis=1)


def backward_kernel(
    values, grad, b_ref, c_ref, run_col, run_row, step_row,
    grad_values, row_sums, col_sums, grad_b, grad_c, scores, grad_scores,
):
    length = values.shape[0]
    width = values.shape[1] // PAIR
    at = pl.program_id(0)

    @pl.when(at == 0)
    def _():
        scores[...] = dot(c_ref[...], b_ref[...], ((1,), (1,)), EXACT)
        grad_scores[...] = jnp.zeros_like(grad_scores)

    parts = []
    for i in range(PAIR):
        lanes = slice(i * width, (i + 1) * width)
        step = step_row[0, i : i + 1, :]
        gout = grad[:, lanes]
        grad_weight = dot(gout, values[:, lanes], ((1,), (1,)), EXACT)
        decays = spread_of(run_col[0, :, i : i + 1], run_row[0, i : i + 1, :], length)
        scored = scores[...] * decays
        weight = scored * step
        parts.append(dot(weight.astype(LOW), gout.astype(LOW), ((0,), (0,))))
        terms = grad_weight * scored
        col_sums[0, i : i + 1, :] = jnp.sum(terms, axis=0, keepdims=True)
        row_sums[0, :, i : i + 1] = jnp.sum(terms * step, axis=1, keepdims=True)
        grad_scores[...] += grad_weight * decays * step
    grad_values[...] = jnp.concatenate(parts, axis=1)

    @pl.when(at == pl.num_programs(0) - 1)
    def _():
        total = grad_scores[...]
        grad_c[...] = dot(total, b_ref[...], ((1,), (0,)), EXACT)
        grad_b[...] = dot(total, c_ref[...], ((0,), (0,)), EXACT)


def specs(length, lanes, state, first_b):
    block = pl.BlockSpec((length, lanes), lambda i: (0, i))
    b_spec = pl.BlockSpec((length, state), lambda i: (0, first_b))
    c_spec = pl.BlockSpec((length, state), lambda i: (0, first_b + 1))
    col = pl.BlockSpec((1, length, PAIR), lambda i: (i, 0, 0))
    row = pl.BlockSpec((1, PAIR, length), lambda i: (i, 0, 0))
    return block, b_spec, c_spec, col, row


def as_cols(a):
    length, heads = a.shape
    return a.reshape(length, heads // PAIR, PAIR).transpose(1, 0, 2)


def as_rows(a):
    length, heads = a.shape
    return a.T.reshape(heads // PAIR, PAIR, length)


def shifted(a, by):
    if by == 0:
        return a
    zeros = jnp.zeros((abs(by), a.shape[1]), a.dtype)
    if by > 0:
        return jnp.concatenate([zeros, a[:-by]], axis=0)
    return jnp.concatenate([a[-by:], zeros], axis=0)


def mixer_forward(projected, conv_weight, conv_bias, dt_bias, a_log, skip_gain, gate_gain):
    length = projected.shape[0]
    inner = gate_gain.shape[0]
    heads = skip_gain.shape[0]
    channels = conv_bias.shape[0]
    state = (channels - inner) // 2
    taps = conv_weight.shape[0]
    lanes = inner // heads * PAIR
    gate_in = projected[:, :inner]
    conv_in = projected[:, inner : inner + channels]
    step_in = projected[:, inner + channels :] + dt_bias
    convolved = conv_bias
    for k in range(taps):
        convolved = convolved + conv_weight[k] * shifted(conv_in, taps - 1 - k)
    active = convolved * jax.nn.sigmoid(convolved)
    step = jax.nn.softplus(step_in)
    rate = -jnp.exp(a_log)
    ids = jnp.arange(length)
    lower = (ids[:, None] >= ids[None, :]).astype(F32)
    running = dot(lower, step * rate, ((1,), (0,)), EXACT)
    packed = (as_cols(running), as_rows(running), as_rows(step))
    block, b_spec, c_spec, col, row = specs(length, lanes, state, inner // state)
    scan = pl.pallas_call(
        forward_kernel,
        grid=(heads // PAIR,),
        in_specs=[block, b_spec, c_spec, col, row, row],
        out_specs=block,
        out_shape=jax.ShapeDtypeStruct((length, inner), F32),
        scratch_shapes=[pltpu.VMEM((length, length), F32)],
        cost_estimate=pl.CostEstimate(
            flops=2 * length * length * inner,
            bytes_accessed=8 * length * inner,
            transcendentals=length * length * heads,
        ),
        name="scan_forward",
    )(active, active, active, *packed)
    values = active[:, :inner]
    skip = jnp.repeat(skip_gain, inner // heads)
    scanned = scan + skip * values
    gated = scanned * (gate_in * jax.nn.sigmoid(gate_in))
    scale = lax.rsqrt(jnp.mean(gated * gated, axis=-1, keepdims=True) + EPS)
    mixed = (gated * scale * gate_gain).astype(LOW)
    saved = (gate_in, conv_in, step_in, convolved, active, step, rate, lower, packed, scanned, scale, skip)
    return mixed, saved


def silu_slope(v):
    s = jax.nn.sigmoid(v)
    return s * (1.0 + v * (1.0 - s))


def mixer_backward(saved, grad_mixed, conv_weight, gate_gain):
    gate_in, conv_in, step_in, convolved, active, step, rate, lower, packed, scanned, scale, skip = saved
    length, inner = gate_in.shape
    heads = step.shape[1]
    channels = conv_in.shape[1]
    state = (channels - inner) // 2
    taps = conv_weight.shape[0]
    lanes = inner // heads * PAIR
    silu_gate = gate_in * jax.nn.sigmoid(gate_in)
    gated = scanned * silu_gate
    grad_gain = jnp.sum(grad_mixed * gated * scale, axis=0)
    scaled = grad_mixed * gate_gain
    along = jnp.mean(scaled * gated, axis=-1, keepdims=True)
    grad_gated = scale * scaled - gated * (scale * scale * scale * along)
    grad_gate_in = grad_gated * scanned * silu_slope(gate_in)
    grad_scanned = grad_gated * silu_gate
    values = active[:, :inner]
    grad_skip = jnp.sum(jnp.sum(grad_scanned * values, axis=0).reshape(heads, -1), axis=1)
    block, b_spec, c_spec, col, row = specs(length, lanes, state, inner // state)
    whole = pl.BlockSpec((length, state), lambda i: (0, 0))
    grad_values, row_sums, col_sums, grad_b, grad_c = pl.pallas_call(
        backward_kernel,
        grid=(heads // PAIR,),
        in_specs=[block, block, b_spec, c_spec, col, row, row],
        out_specs=[block, col, row, whole, whole],
        out_shape=[
            jax.ShapeDtypeStruct((length, inner), F32),
            jax.ShapeDtypeStruct((heads // PAIR, length, PAIR), F32),
            jax.ShapeDtypeStruct((heads // PAIR, PAIR, length), F32),
            jax.ShapeDtypeStruct((length, state), F32),
            jax.ShapeDtypeStruct((length, state), F32),
        ],
        scratch_shapes=[pltpu.VMEM((length, length), F32), pltpu.VMEM((length, length), F32)],
        cost_estimate=pl.CostEstimate(
            flops=4 * length * length * inner,
            bytes_accessed=12 * length * inner,
            transcendentals=length * length * heads,
        ),
        name="scan_backward",
    )(active, grad_scanned, active, active, *packed)
    by_row = row_sums.transpose(1, 0, 2).reshape(length, heads)
    by_col = col_sums.reshape(heads, length).T
    grad_running = by_row - by_col * step
    grad_decay = dot(lower, grad_running, ((0,), (0,)), EXACT)
    grad_a_log = jnp.sum(grad_decay * step, axis=0) * rate
    grad_step_in = (by_col + grad_decay * rate) * jax.nn.sigmoid(step_in)
    grad_dt = jnp.sum(grad_step_in, axis=0)
    grad_active = jnp.concatenate([grad_values + grad_scanned * skip, grad_b, grad_c], axis=1)
    grad_conv = grad_active * silu_slope(convolved)
    grad_conv_in = sum(
        conv_weight[k] * shifted(grad_conv, -(taps - 1 - k)) for k in range(taps)
    )
    grad_conv_w = jnp.stack(
        [jnp.sum(grad_conv * shifted(conv_in, taps - 1 - k), axis=0) for k in range(taps)]
    )
    grad_conv_b = jnp.sum(grad_conv, axis=0)
    grad_proj = jnp.concatenate(
        [grad_gate_in.astype(LOW), grad_conv_in.astype(LOW), grad_step_in.astype(LOW)], axis=1
    )
    return grad_proj, (grad_conv_w, grad_conv_b, grad_dt, grad_a_log, grad_skip, grad_gain)


def by_sequence(items):
    return items[0] if len(items) == 1 else jnp.concatenate(items, axis=0)


def reduced(grad_in, grad_out):
    depth, proj = grad_in.shape
    folded = grad_out.astype(LOW).reshape(depth, -1)
    joined = jnp.concatenate([folded, grad_in.astype(LOW)], axis=1)
    half = lax.psum_scatter(joined, ("dp", "rep"), scatter_dimension=0, tiled=True)
    owned = lax.all_gather(half, "rep", axis=0, tiled=True).astype(F32)
    cut = folded.shape[1]
    return owned[:, cut:], owned[:, :cut].reshape(-1, grad_out.shape[1])


def local(
    inputs, norm_gain, in_weight, conv_weight, conv_bias, dt_bias, a_log,
    skip_gain, gate_gain, out_weight, cotangent,
):
    seqs, length, model = inputs.shape
    rows = seqs * length
    in_full = lax.all_gather(in_weight, "dp", axis=0, tiled=True)
    out_full = lax.all_gather(out_weight, "dp", axis=0, tiled=True)
    rows_in = inputs.astype(F32).reshape(rows, model)
    front = lax.rsqrt(jnp.mean(rows_in * rows_in, axis=-1, keepdims=True) + EPS)
    normed = (rows_in * front * norm_gain).astype(LOW)
    projected = dot(normed, in_full, ((1,), (0,)))
    cot = cotangent.reshape(rows, model)

    saved = []
    mixed = []
    for s in range(seqs):
        part, keep = mixer_forward(
            projected[s * length : (s + 1) * length],
            conv_weight, conv_bias, dt_bias, a_log, skip_gain, gate_gain,
        )
        mixed.append(part)
        saved.append(keep)
    mixed = by_sequence(mixed)
    grad_out = dot(mixed, cot, ((0,), (0,)))
    output = (rows_in + dot(mixed, out_full, ((1,), (0,)))).astype(LOW).reshape(inputs.shape)
    grad_mixed = dot(cot, out_full, ((1,), (1,)))

    grad_proj = []
    totals = None
    for s in range(seqs):
        part, sums = mixer_backward(
            saved[s], grad_mixed[s * length : (s + 1) * length], conv_weight, gate_gain
        )
        grad_proj.append(part)
        totals = sums if totals is None else tuple(a + b for a, b in zip(totals, sums))
    grad_proj = by_sequence(grad_proj)
    grad_in, grad_out = reduced(dot(normed, grad_proj, ((0,), (0,))), grad_out)
    grad_normed = dot(grad_proj, in_full, ((1,), (1,)))
    grad_norm = jnp.sum(grad_normed * rows_in * front, axis=0)
    scaled = grad_normed * norm_gain
    along = jnp.mean(scaled * rows_in, axis=-1, keepdims=True)
    grad_rows = front * scaled - rows_in * (front * front * front * along)
    grad_inputs = (cot.astype(F32) + grad_rows).astype(LOW).reshape(inputs.shape)

    smalls = (grad_norm,) + totals
    flat = lax.psum(jnp.concatenate([a.reshape(-1) for a in smalls]), ("dp", "rep"))
    summed = []
    at = 0
    for a in smalls:
        summed.append(flat[at : at + a.size].reshape(a.shape))
        at += a.size
    return (output, grad_inputs, summed[0], grad_in) + tuple(summed[1:]) + (grad_out,)


def solution(mesh):
    rows = P(("dp", "rep"), None, None)
    owned = P("dp", None)
    return jax.shard_map(
        local,
        mesh=mesh,
        in_specs=(rows, P(), owned, P(), P(), P(), P(), P(), P(), owned, rows),
        out_specs=(rows, rows, P(), owned, P(), P(), P(), P(), P(), P(), owned),
        check_vma=False,
    )
```

time: 719 us -> 372 us (0.52)
  matrix products: 198 us -> 25.6 us
  other arithmetic: 151 us -> 35.1 us
  local copies, waits for them, and re-layouts: 155 us -> 44.9 us
  waiting for transfers between devices: 139 us -> 176 us
  Pallas kernels: 0 us -> 25.8 us
    dot_general x130 -> x8, matrix products: 198 us -> 25.6 us  [dot(): lax.dot_general(a, b, (dims, ((), ())), precision=precision, preferred_el...]
    squeeze x72 -> x0, local copies, waits for them, and re-layouts: 74.2 us -> none  [mixer(): lax.map(jax.checkpoint(one_head), (head_values, head_steps, decay_rate))]
    another operation x144 -> x1, other arithmetic: 58 us -> 0.03 us  [mixer_backward(): jnp.stack([jnp.sum(grad_conv * shifted(conv_in, taps - 1 - k), axis=0) fo...]
    unnamed x5 -> x4, waiting for transfers between devices: 82.3 us -> 116 us
    mul x51 -> x4, other arithmetic: 36.6 us -> 5.64 us  [the longest x1 5.62 us: mixer_forward(): active = convolved * jax.nn.sigmoid(convolved)]
    dynamic_slice x48 -> x0, local copies, waits for them, and re-layouts: 28 us -> none  [mixer(): lax.map(jax.checkpoint(one_head), (head_values, head_steps, decay_rate))]
    pallas_call x0 -> x2, Pallas kernels: none -> 25.8 us  [the longest x1 15.2 us: mixer_backward(): pl.pallas_call(backward_kernel, grid=(heads // PAIR,), in_specs=[block, b...]
    another operation x219 -> x4, local copies, waits for them, and re-layouts: 20.5 us -> 0.03 us  [mixer_backward(): jnp.stack([jnp.sum(grad_conv * shifted(conv_in, taps - 1 - k), axis=0) fo...]
  transfers between devices with their start and end apart: 4 -> 3, of which waited for: 2 -> 3; matrix products, arithmetic and copies ran while one was open for 69% -> 13% of each run, Pallas kernels for 0% -> 3%
where the time goes in v1:
time: 372 us; the launch traced here: 371 us
  waiting for transfers between devices  176 us (47%)
  blocking collectives  48.9 us (13%)
  local copies, waits for them, and re-layouts  44.9 us (12%)
  other arithmetic  35.1 us (9%)
  Pallas kernels  25.8 us (7%)
  matrix products  25.6 us (7%)
  between operations  14.1 us (4%)
    unnamed x4, waiting for transfers between devices  116 us
    all_gather x1, waiting for transfers between devices, local(): in_full = lax.all_gather(in_weight, 'dp', axis=0, tiled=True)  55.2 us
    psum x1, blocking collectives, local(): lax.psum(jnp.concatenate([a.reshape(-1) for a in smalls]), ('dp', 'rep'))  40.5 us
    dot_general x8, matrix products, dot(): lax.dot_general(a, b, (dims, ((), ())), precision=precision, preferred_el...  25.6 us
    pallas_call x1, Pallas kernels, mixer_backward(): pl.pallas_call(backward_kernel, grid=(heads // PAIR,), in_specs=[block, b...  15.2 us
    pallas_call x1, Pallas kernels, mixer_forward(): pl.pallas_call(forward_kernel, grid=(heads // PAIR,), in_specs=[block, b_...  10.6 us
    reshape x2, local copies, waits for them, and re-layouts, reduced(): folded = grad_out.astype(LOW).reshape(depth, -1)  9.02 us
    all_gather x1, blocking collectives, reduced(): owned = lax.all_gather(half, 'rep', axis=0, tiled=True).astype(F32)  8.36 us
  transfers between devices with their start and end apart: 3, of which 3 were waited for; matrix products, arithmetic and copies ran while one was open for 13% of the time, Pallas kernels for 3%

profile of v1, /device:TPU:0, one launch (start us, length us, event | category | flops | bytes accessed | tf_op | source)
XLA Modules:
  0.0 370.7 jit_solution(8627763869040227330)
XLA Ops:
  9.5 1.6 slice_reduce_fusion.3
  11.1 1.2 fusion.4
  12.2 1.2 exponential_negate_fusion
  14.0 55.2 %all-gather.3.cloned.1.call-done = bf16[768,3352]{1,0:T(8,128)(2,1)} async-done(((bf16[48,3352]{1,0:T(8,128)(2,1)}), bf16[768,3352]{1,0:T(8,128)(2,1)}) %all-gather.3.cloned.1.call-update) | async-done | bytes 5148688 | tf_op jit(solution)/shard_map/all_gather | solution.py:241
  69.2 4.3 %fusion.27 = f32[256,3352]{1,0:T(8,128)S(1)} fusion(bf16[768,3352]{1,0:T(8,128)(2,1)} %all-gather.3.cloned.1.call-done, bf16[1,256,768]{2,1,0:T(8,128)(2,1)} %param.11, f32[768]{0:T(1024)} %param.12, f32[256]{0:T(256)} %add_rsqrt_fusion.1), kind=kOutput, calls=%fused_computation.59 | convolution fusion | flops 1318846464 | bytes 8978432 | tf_op jit(solution)/shard_map/dot_general | solution.py:16
  73.6 1.5 slice.105
  75.1 1.4 slice.104
  76.5 1.3 slice.103
  77.8 0.9 fusion.21
  78.8 1.4 reshape.115
  80.1 2.4 copy.87
  82.5 1.4 reshape.116.run_row
  83.9 1.4 fusion.35
  85.3 1.6 copy.88
  86.9 1.4 reshape.117.step_row
  88.2 5.6 %fusion = (f32[256,1792]{1,0:T(8,128)}, f32[256,1792]{1,0:T(8,128)}) fusion(f32[256,3352]{1,0:T(8,128)S(1)} %fusion.27, f32[1792]{0:T(1024)} %get-tuple-element.54, f32[255,1792]{1,0:T(8,128)} %slice.105, f32[1792]{0:T(1024)} %get-tuple-element.55, f32[254,1792]{1,0:T(8,128)} %slice.104, f32[1792]{0:T(1024)} %get-tuple-element.53, f32[253,1792]{1,0:T(8,128)} %slice.103, ...), kind=kLoop, calls=%fused_computation.10 | loop fusion | flops 5505024 | bytes 11002880 | tf_op jit(solution)/shard_map/mul | solution.py:122
  93.9 10.6 %scan_forward.1 = f32[256,1536]{1,0:T(8,128)} custom-call(f32[256,1792]{1,0:T(8,128)} %get-tuple-element.63.values.b_ref.c_ref, f32[256,1792]{1,0:T(8,128)} %get-tuple-element.63.values.b_ref.c_ref, f32[256,1792]{1,0:T(8,128)} %get-tuple-element.63.values.b_ref.c_ref, f32[12,256,2]{2,1,0:T(8,128)} %bitcast.48, f32[12,2,256]{2,1,0:T(2,128)} %reshape.116.run_row, ...), custom_call_target="tpu_custom_call" | custom-call | flops 201326592 | bytes 3145728 | tf_op jit(solution)/shard_map/scan_forward/pallas_call | solution.py:130
  104.5 2.5 multiply_reduce_fusion.7
  107.0 5.4 %all-gather.5.cloned.1.call-done = bf16[1536,768]{1,0:T(8,128)(2,1)} async-done(((bf16[96,768]{1,0:T(8,128)(2,1)}), bf16[1536,768]{1,0:T(8,128)(2,1)}) %all-gather.5.cloned.1.call-update) | async-done | bytes 2359312 | tf_op jit(solution)/shard_map/all_gather | solution.py:242
  112.5 3.5 multiply_reduce_fusion.4
  115.9 4.7 %multiply_reduce_fusion.5 = (f32[1536]{0:T(1024)}, f32[256,1536]{1,0:T(8,128)}, bf16[256,1536]{1,0:T(8,128)(2,1)}) fusion(f32[256,1792]{1,0:T(8,128)S(1)} %copy-done, f32[256,3352]{1,0:T(8,128)} %copy-done.1, f32[256,1536]{1,0:T(8,128)S(1)} %get-tuple-element.62, f32[256]{0:T(256)S(1)} %fusion.30, f32[256,1536]{1,0:T(8,128)S(1)} %get-tuple-element.70, ...), kind=kLoop, calls=%fused_computation.20 | loop fusion | flops 7862784 | bytes 10244096 | tf_op jit(solution)/shard_map/reduce_sum | solution.py:176
  120.6 15.2 %scan_backward.1 = (f32[256,1536]{1,0:T(8,128)}, f32[12,256,2]{2,1,0:T(8,128)}, f32[12,2,256]{2,1,0:T(2,128)}, f32[256,128]{1,0:T(8,128)}, f32[256,128]{1,0:T(8,128)}) custom-call(f32[256,1792]{1,0:T(8,128)} %get-tuple-element.63.values.b_ref.c_ref, f32[256,1536]{1,0:T(8,128)} %get-tuple-element.57.grad, f32[256,1792]{1,0:T(8,128)} %get-tuple-element.63.values.b_ref.c_ref, ...), custom_call_target="tpu_custom_call" | custom-call | flops 402653184 | bytes 4718592 | tf_op jit(solution)/shard_map/scan_backward/pallas_call | solution.py:179
  135.9 1.8 multiply_add_fusion.1
  138.3 4.7 %fusion.36 = (f32[1792]{0:T(1024)}, f32[1792]{0:T(1024)}, f32[1792]{0:T(1024)}, f32[1792]{0:T(1024)}, f32[1792]{0:T(1024)}, /*index=5*/f32[256,1792]{1,0:T(8,128)S(1)}) fusion(f32[256,3352]{1,0:T(8,128)S(1)} %copy-done.2, f32[255,1792]{1,0:T(8,128)} %slice.105, f32[254,1792]{1,0:T(8,128)} %slice.104, f32[253,1792]{1,0:T(8,128)} %slice.103, ...), kind=kLoop, calls=%fused_computation.78 | loop fusion | flops 8707328 | bytes 12837888 | tf_op jit(solution)/shard_map/reduce_sum | solution.py:214
  143.0 1.5 slice.112
  144.5 1.4 slice.111
  145.8 1.3 slice.110
  147.2 2.4 convolution_convert_fusion.1
  150.2 0.8 copy.90
  151.0 2.5 copy.91
  153.5 1.4 reshape.121
  154.8 1.5 copy.92
  156.3 4.7 %reshape.125 = bf16[768,1536]{1,0:T(8,128)(2,1)} reshape(bf16[1536,768]{1,0:T(8,128)(2,1)} %convolution_convert_fusion.1) | data formatting | bytes 4718592 | tf_op jit(solution)/shard_map/reshape | solution.py:227
  161.1 4.3 %copy.95 = bf16[768,1536]{0,1:T(8,128)(2,1)} copy(bf16[768,1536]{1,0:T(8,128)(2,1)} %reshape.125) | data formatting | bytes 4718592 | tf_op jit(solution)/shard_map/reshape | solution.py:227
  165.4 2.0 fusion.38
  167.4 3.2 add_convert_fusion
  170.6 1.0 copy-done.10
  171.6 3.9 %convolution_convert_fusion = bf16[768,3352]{0,1:T(8,128)(2,1)} fusion(bf16[256,24]{1,0:T(8,128)(2,1)S(1)} %get-tuple-element.59, bf16[256,1792]{1,0:T(8,128)(2,1)S(1)} %add_convert_fusion, bf16[256,1536]{1,0:T(8,128)(2,1)S(1)} %copy-done.12, bf16[1,256,768]{2,1,0:T(8,128)(2,1)S(1)} %copy-done.8, f32[768]{0:T(1024)S(1)} %copy-done.28, f32[256]{0:T(256)S(1)} %copy-done.29), kind=kOutput, calls=%fused_computation.1 | convolution fusion | flops 1326569472 | bytes 7262208 | tf_op jit(solution)/shard_map/dot_general | solution.py:16
  175.5 5.9 %pad_maximum_fusion = bf16[768,4888]{0,1:T(8,128)(2,1)} fusion(bf16[768,3352]{0,1:T(8,128)(2,1)} %convolution_convert_fusion, bf16[768,1536]{0,1:T(8,128)(2,1)S(1)} %copy-done.5), kind=kLoop, calls=%fused_computation | loop fusion | flops 15015936 | bytes 15015936 | tf_op jit(solution)/shard_map/concatenate | solution.py:228
  182.9 5.4 %fusion.12 = (f32[768]{0:T(1024)S(1)}, f32[256]{0:T(256)S(1)}, f32[256,768]{1,0:T(8,128)}) fusion(bf16[1,256,768]{2,1,0:T(8,128)(2,1)S(1)} %copy-done.9, f32[256]{0:T(256)S(1)} %copy-done.29, f32[768]{0:T(1024)S(1)} %copy-done.28, bf16[768,3352]{1,0:T(8,128)(2,1)} %all-gather.3.cloned.1.call-done, bf16[256,24]{1,0:T(8,128)(2,1)S(1)} %copy-done.36, ...), kind=kOutput, calls=%fused_computation.40 | convolution fusion | flops 1324583936 | bytes 8052736 | tf_op jit(solution)/shard_map/dot_general | solution.py:16
  188.4 40.5 %psum.7 = f32[11336]{0:T(1024)S(1)} all-reduce(f32[11336]{0:T(1024)S(1)} %concatenate.41), channel_id=1, replica_groups=mesh['dp'=16,'rep'=2] {'dp','rep'}, use_global_device_ids=true, to_apply=%region_15.16 | all-reduce | flops 11336 | bytes 90688 | tf_op jit(solution)/shard_map/psum | solution.py:281
  232.0 2.1 fusion.16
  234.2 3.2 fusion.3
  237.4 114.2 %all-reduce.9.cloned.1.call-done = bf16[768,4888]{0,1:T(8,128)(2,1)} async-done(((bf16[768,4888]{0,1:T(8,128)(2,1)}), bf16[768,4888]{0,1:T(8,128)(2,1)}) %all-reduce.9.cloned.1.call-update) | async-done | bytes 7507984
  351.6 2.2 constant_dynamic-slice_fusion
  354.2 8.4 %all_gather.11 = bf16[48,4888]{1,0:T(8,128)(2,1)S(1)} all-gather(bf16[24,4888]{1,0:T(8,128)(2,1)S(1)} %copy.96), channel_id=1, replica_groups=mesh['dp'=16,'rep'=2] {'rep'}, dimensions={0}, use_global_device_ids=true | all-gather | bytes 703872 | tf_op jit(solution)/shard_map/all_gather | solution.py:230
  362.5 0.9 slice.114
  363.4 0.8 reshape.127
  (104 shorter events, 9.1 us)
Async XLA Ops:
  7.2 62.1 %all-gather.3.cloned.1.call-start = ((), (), s32[]{:S(2)}) async-start(), calls=%async_computation | async-start | bytes 5640192 | tf_op jit(solution)/shard_map/all_gather | solution.py:241
  7.9 104.5 %all-gather.5.cloned.1.call-start = ((), (), s32[]{:S(2)}) async-start(), calls=%async_computation.1 | async-start | bytes 2506752 | tf_op jit(solution)/shard_map/all_gather | solution.py:242
  8.7 342.9 %all-reduce.9.cloned.1.call-start = ((), (), s32[]{:S(2)}) async-start(), calls=%async_computation.2 | async-start | bytes 15015936
  12.2 1.2 copy-start.26
  73.6 14.7 %copy-start.1 = (f32[256,3352]{1,0:T(8,128)}, f32[256,3352]{1,0:T(8,128)S(1)}, u32[]{:S(2)}) copy-start(f32[256,3352]{1,0:T(8,128)S(1)} %fusion.27) | copy-start | bytes 10297348
  76.5 1.3 copy-start.30
  76.5 1.3 copy-start.34
  93.9 10.7 %copy-start = (f32[256,1792]{1,0:T(8,128)S(1)}, f32[256,1792]{1,0:T(8,128)}, u32[]{:S(2)}) copy-start(f32[256,1792]{1,0:T(8,128)} %get-tuple-element.63.values.b_ref.c_ref) | copy-start | bytes 5505028
  104.5 7.9 %copy-start.13 = (f32[1536]{0:T(1024)S(1)}, f32[1536]{0:T(1024)}, u32[]{:S(2)}) copy-start(f32[1536]{0:T(1024)} %param.19) | copy-start | bytes 18436
  107.0 40.1 %copy-start.16 = (f32[256]{0:T(256)}, f32[256]{0:T(256)S(1)}, u32[]{:S(2)}) copy-start(f32[256]{0:T(256)S(1)} %add_rsqrt_fusion) | copy-start | bytes 3076
  112.5 3.5 copy-start.3
  120.6 15.2 %copy-start.4 = (f32[256,1536]{1,0:T(8,128)S(1)}, f32[256,1536]{1,0:T(8,128)}, u32[]{:S(2)}) copy-start(f32[256,1536]{1,0:T(8,128)} %get-tuple-element.57.grad) | copy-start | bytes 4718596
  135.8 2.5 copy-start.2
  135.9 2.5 copy-start.14
  135.9 2.5 copy-start.15
  145.8 1.3 copy-start.6
  147.2 2.4 copy-start.25
  167.4 3.2 copy-start.35
  167.4 4.2 %copy-start.8 = (bf16[1,256,768]{2,1,0:T(8,128)(2,1)S(1)}, bf16[1,256,768]{2,1,0:T(8,128)(2,1)}, u32[]{:S(2)}) copy-start(bf16[1,256,768]{2,1,0:T(8,128)(2,1)} %param.11) | copy-start | bytes 1179652
  167.4 4.2 %copy-start.12 = (bf16[256,1536]{1,0:T(8,128)(2,1)S(1)}, bf16[256,1536]{1,0:T(8,128)(2,1)}, u32[]{:S(2)}) copy-start(bf16[256,1536]{1,0:T(8,128)(2,1)} %get-tuple-element.65) | copy-start | bytes 2359300
  167.4 4.2 %copy-start.28 = (f32[768]{0:T(1024)S(1)}, f32[768]{0:T(1024)}, u32[]{:S(2)}) copy-start(f32[768]{0:T(1024)} %param.12) | copy-start | bytes 9220
  167.4 4.2 %copy-start.29 = (f32[256]{0:T(256)S(1)}, f32[256]{0:T(256)}, u32[]{:S(2)}) copy-start(f32[256]{0:T(256)} %add_rsqrt_fusion.1) | copy-start | bytes 3076
  170.6 1.0 copy-start.10
  171.6 3.9 %copy-start.5 = (bf16[768,1536]{0,1:T(8,128)(2,1)S(1)}, bf16[768,1536]{0,1:T(8,128)(2,1)}, u32[]{:S(2)}) copy-start(bf16[768,1536]{0,1:T(8,128)(2,1)} %copy.95) | copy-start | bytes 7077892
  181.4 0.7 copy-start.24
  181.4 0.7 copy-start.23
  181.4 0.7 copy-start.22
  181.4 0.7 copy-start.21
  181.4 0.8 copy-start.19
  181.4 1.0 copy-start.32
  181.5 1.0 copy-start.33
  181.5 1.1 copy-start.9
  181.5 1.4 copy-start.11
  181.5 1.3 copy-start.36
  182.8 5.4 %copy-start.18 = (f32[1536]{0:T(1024)S(1)}, f32[1536]{0:T(1024)}, u32[]{:S(2)}) copy-start(f32[1536]{0:T(1024)} %get-tuple-element.43) | copy-start | bytes 18436
  182.8 5.4 %copy-start.20 = (f32[1792]{0:T(1024)S(1)}, f32[1792]{0:T(1024)}, u32[]{:S(2)}) copy-start(f32[1792]{0:T(1024)} %get-tuple-element.45) | copy-start | bytes 21508
  182.8 5.4 %copy-start.31 = (f32[24]{0:T(128)S(1)}, f32[24]{0:T(128)}, u32[]{:S(2)}) copy-start(f32[24]{0:T(128)} %get-tuple-element.58) | copy-start | bytes 292
  182.8 48.6 %copy-start.27 = (f32[256]{0:T(256)S(1)}, f32[256]{0:T(256)}, u32[]{:S(2)}) copy-start(f32[256]{0:T(256)} %copy-done.26) | copy-start | bytes 3076
  182.9 49.2 %copy-start.7 = (bf16[1,256,768]{2,1,0:T(8,128)(2,1)S(1)}, bf16[1,256,768]{2,1,0:T(8,128)(2,1)}, u32[]{:S(2)}) copy-start(bf16[1,256,768]{2,1,0:T(8,128)(2,1)} %param.21) | copy-start | bytes 1179652
  188.3 45.9 %copy-start.17 = (f32[256]{0:T(256)S(1)}, f32[256]{0:T(256)}, u32[]{:S(2)}) copy-start(f32[256]{0:T(256)} %copy-done.16) | copy-start | bytes 3076
Sparse Core Ops, SparseCore 0:
  10.2 59.0 all-gather.2
  71.5 40.9 all-gather.4
  181.6 169.8 all-reduce.8

commit v2 on v1

--- a/solution.py
+++ b/solution.py
@@ -222,14 +222,9 @@
     return items[0] if len(items) == 1 else jnp.concatenate(items, axis=0)
 
 
-def reduced(grad_in, grad_out):
-    depth, proj = grad_in.shape
-    folded = grad_out.astype(LOW).reshape(depth, -1)
-    joined = jnp.concatenate([folded, grad_in.astype(LOW)], axis=1)
-    half = lax.psum_scatter(joined, ("dp", "rep"), scatter_dimension=0, tiled=True)
-    owned = lax.all_gather(half, "rep", axis=0, tiled=True).astype(F32)
-    cut = folded.shape[1]
-    return owned[:, cut:], owned[:, :cut].reshape(-1, grad_out.shape[1])
+def reduced(grad):
+    half = lax.psum_scatter(grad.astype(LOW), ("dp", "rep"), scatter_dimension=0, tiled=True)
+    return lax.all_gather(half, "rep", axis=0, tiled=True).astype(F32)
 
 
 def local(
@@ -256,7 +251,7 @@
         mixed.append(part)
         saved.append(keep)
     mixed = by_sequence(mixed)
-    grad_out = dot(mixed, cot, ((0,), (0,)))
+    grad_out = reduced(dot(mixed, cot, ((0,), (0,))))
     output = (rows_in + dot(mixed, out_full, ((1,), (0,)))).astype(LOW).reshape(inputs.shape)
     grad_mixed = dot(cot, out_full, ((1,), (1,)))
 
@@ -269,7 +264,7 @@
         grad_proj.append(part)
         totals = sums if totals is None else tuple(a + b for a, b in zip(totals, sums))
     grad_proj = by_sequence(grad_proj)
-    grad_in, grad_out = reduced(dot(normed, grad_proj, ((0,), (0,))), grad_out)
+    grad_in = reduced(dot(normed, grad_proj, ((0,), (0,))))
     grad_normed = dot(grad_proj, in_full, ((1,), (1,)))
     grad_norm = jnp.sum(grad_normed * rows_in * front, axis=0)
     scaled = grad_normed * norm_gain

time: 372 us -> 339 us (0.911)
  waiting for transfers between devices: 176 us -> 160 us
  local copies, waits for them, and re-layouts: 44.9 us -> 30.4 us
  other arithmetic: 35.1 us -> 30.7 us
    unnamed x4 -> x5, waiting for transfers between devices: 116 us -> 102 us
    reshape x3 -> x0, local copies, waits for them, and re-layouts: 9.78 us -> none  [the longest x2 9.02 us: reduced(): folded = grad_out.astype(LOW).reshape(depth, -1)]
    concatenate x1 -> x0, other arithmetic: 5.95 us -> none  [reduced(): joined = jnp.concatenate([folded, grad_in.astype(LOW)], axis=1)]
    all_gather x1 -> x2, blocking collectives: 8.36 us -> 11.7 us  [reduced(): return lax.all_gather(half, 'rep', axis=0, tiled=True).astype(F32)]
  transfers between devices with their start and end apart: 3 -> 4, of which waited for: 3 -> 3; matrix products, arithmetic and copies ran while one was open for 13% -> 25% of each run, Pallas kernels for 3% -> 8%
where the time goes in v2:
time: 339 us; the launch traced here: 338 us
  waiting for transfers between devices  160 us (47%)
  blocking collectives  50.8 us (15%)
  other arithmetic  30.7 us (9%)
  local copies, waits for them, and re-layouts  30.4 us (9%)
  matrix products  25.9 us (8%)
  Pallas kernels  25.8 us (8%)
  between operations  14.1 us (4%)
    unnamed x5, waiting for transfers between devices  102 us
    all_gather x1, waiting for transfers between devices, local(): in_full = lax.all_gather(in_weight, 'dp', axis=0, tiled=True)  55.2 us
    psum x1, blocking collectives, local(): lax.psum(jnp.concatenate([a.reshape(-1) for a in smalls]), ('dp', 'rep'))  39.2 us
    dot_general x8, matrix products, dot(): lax.dot_general(a, b, (dims, ((), ())), precision=precision, preferred_el...  25.9 us
    pallas_call x1, Pallas kernels, mixer_backward(): pl.pallas_call(backward_kernel, grid=(heads // PAIR,), in_specs=[block, b...  15.3 us
    all_gather x2, blocking collectives, reduced(): return lax.all_gather(half, 'rep', axis=0, tiled=True).astype(F32)  11.7 us
    pallas_call x1, Pallas kernels, mixer_forward(): pl.pallas_call(forward_kernel, grid=(heads // PAIR,), in_specs=[block, b_...  10.5 us
  transfers between devices with their start and end apart: 4, of which 3 were waited for; matrix products, arithmetic and copies ran while one was open for 25% of the time, Pallas kernels for 8%

profile of v2, /device:TPU:0, one launch (start us, length us, event | category | flops | bytes accessed | tf_op | source)
XLA Modules:
  0.0 337.9 jit_solution(16578337669639469286)
XLA Ops:
  7.2 0.7 all-gather.3.cloned.1.call-update
  8.0 0.7 all-gather.5.cloned.1.call-update
  8.7 0.7 broadcast_in_dim.2
  9.5 1.6 slice_reduce_fusion.3
  11.1 1.2 fusion.4
  12.2 1.2 exponential_negate_fusion
  14.0 55.2 %all-gather.3.cloned.1.call-done = bf16[768,3352]{1,0:T(8,128)(2,1)} async-done(((bf16[48,3352]{1,0:T(8,128)(2,1)}), bf16[768,3352]{1,0:T(8,128)(2,1)}) %all-gather.3.cloned.1.call-update) | async-done | bytes 5148688 | tf_op jit(solution)/shard_map/all_gather | solution.py:236
  69.2 4.3 %fusion.27 = f32[256,3352]{1,0:T(8,128)S(1)} fusion(bf16[768,3352]{1,0:T(8,128)(2,1)} %all-gather.3.cloned.1.call-done, bf16[1,256,768]{2,1,0:T(8,128)(2,1)} %param.11, f32[768]{0:T(1024)} %param.12, f32[256]{0:T(256)} %add_rsqrt_fusion.1), kind=kOutput, calls=%fused_computation.58 | convolution fusion | flops 1318846464 | bytes 8978432 | tf_op jit(solution)/shard_map/dot_general | solution.py:16
  73.6 1.5 slice.97
  75.0 1.5 slice.96
  76.6 1.3 slice.95
  77.9 0.9 fusion.21
  78.9 1.4 reshape.109
  80.2 1.4 reshape.110.run_row
  81.6 1.4 fusion.35
  83.0 1.6 copy.79
  84.6 1.4 reshape.111.step_row
  85.9 2.4 copy.78
  88.3 5.6 %fusion = (f32[256,1792]{1,0:T(8,128)}, f32[256,1792]{1,0:T(8,128)}) fusion(f32[256,3352]{1,0:T(8,128)S(1)} %fusion.27, f32[1792]{0:T(1024)} %get-tuple-element.32, f32[255,1792]{1,0:T(8,128)} %slice.97, f32[1792]{0:T(1024)} %get-tuple-element.33, f32[254,1792]{1,0:T(8,128)} %slice.96, f32[1792]{0:T(1024)} %get-tuple-element.31, f32[253,1792]{1,0:T(8,128)} %slice.95, ...), kind=kLoop, calls=%fused_computation.9 | loop fusion | flops 5505024 | bytes 11002880 | tf_op jit(solution)/shard_map/mul | solution.py:122
  94.0 10.5 %scan_forward.1 = f32[256,1536]{1,0:T(8,128)} custom-call(f32[256,1792]{1,0:T(8,128)} %get-tuple-element.41.values.b_ref.c_ref, f32[256,1792]{1,0:T(8,128)} %get-tuple-element.41.values.b_ref.c_ref, f32[256,1792]{1,0:T(8,128)} %get-tuple-element.41.values.b_ref.c_ref, f32[12,256,2]{2,1,0:T(8,128)} %bitcast.46, f32[12,2,256]{2,1,0:T(2,128)} %reshape.110.run_row, ...), custom_call_target="tpu_custom_call" | custom-call | flops 201326592 | bytes 3145728 | tf_op jit(solution)/shard_map/scan_forward/pallas_call | solution.py:130
  104.5 2.5 multiply_reduce_fusion.7
  107.1 2.4 convolution_convert_fusion.1
  109.8 2.7 all-gather.5.cloned.1.call-done
  112.5 3.5 %multiply_reduce_fusion.4 = (f32[1536]{0:T(1024)}, f32[256]{0:T(256)S(1)}, f32[256,1536]{1,0:T(8,128)S(1)}) fusion(f32[256,1536]{1,0:T(8,128)S(1)} %get-tuple-element.40, f32[256]{0:T(256)S(1)} %add_rsqrt_fusion, f32[1536]{0:T(1024)S(1)} %copy-done.12, bf16[1536,768]{1,0:T(8,128)(2,1)} %all-gather.5.cloned.1.call-done, bf16[1,256,768]{2,1,0:T(8,128)(2,1)} %param.21), kind=kOutput, calls=%fused_computation.18 | convolution fusion | flops 606337280 | bytes 5912576 | tf_op jit(solution)/shard_map/dot_general | solution.py:16
  115.9 4.5 %multiply_reduce_fusion.5 = (f32[1536]{0:T(1024)}, f32[256,1536]{1,0:T(8,128)}, bf16[256,1536]{1,0:T(8,128)(2,1)}) fusion(f32[256,1792]{1,0:T(8,128)S(1)} %copy-done, f32[256,3352]{1,0:T(8,128)} %copy-done.1, f32[256,1536]{1,0:T(8,128)S(1)} %get-tuple-element.40, f32[256]{0:T(256)S(1)} %fusion.30, f32[256,1536]{1,0:T(8,128)S(1)} %get-tuple-element.48, ...), kind=kLoop, calls=%fused_computation.19 | loop fusion | flops 7862784 | bytes 10244096 | tf_op jit(solution)/shard_map/reduce_sum | solution.py:176
  120.5 15.3 %scan_backward.1 = (f32[256,1536]{1,0:T(8,128)}, f32[12,256,2]{2,1,0:T(8,128)}, f32[12,2,256]{2,1,0:T(2,128)}, f32[256,128]{1,0:T(8,128)}, f32[256,128]{1,0:T(8,128)}) custom-call(f32[256,1792]{1,0:T(8,128)} %get-tuple-element.41.values.b_ref.c_ref, f32[256,1536]{1,0:T(8,128)} %get-tuple-element.35.grad, f32[256,1792]{1,0:T(8,128)} %get-tuple-element.41.values.b_ref.c_ref, ...), custom_call_target="tpu_custom_call" | custom-call | flops 402653184 | bytes 4718592 | tf_op jit(solution)/shard_map/scan_backward/pallas_call | solution.py:179
  135.8 1.8 multiply_add_fusion.1
  138.3 4.8 %fusion.36 = (f32[1792]{0:T(1024)}, f32[1792]{0:T(1024)}, f32[1792]{0:T(1024)}, f32[1792]{0:T(1024)}, f32[1792]{0:T(1024)}, /*index=5*/f32[256,1792]{1,0:T(8,128)S(1)}) fusion(f32[256,3352]{1,0:T(8,128)S(1)} %copy-done.2, f32[255,1792]{1,0:T(8,128)} %slice.97, f32[254,1792]{1,0:T(8,128)} %slice.96, f32[253,1792]{1,0:T(8,128)} %slice.95, ...), kind=kLoop, calls=%fused_computation.76 | loop fusion | flops 8707328 | bytes 12837888 | tf_op jit(solution)/shard_map/reduce_sum | solution.py:214
  143.1 1.4 slice.104
  144.5 1.4 slice.103
  145.9 1.4 slice.102
  147.9 1.9 copy.82
  150.4 0.8 copy.83
  151.3 1.5 copy.81
  152.8 2.1 fusion.38
  154.9 3.2 add_convert_fusion
  158.1 0.9 copy-done.9
  159.0 4.0 %convolution_convert_fusion = bf16[768,3352]{1,0:T(8,128)(2,1)} fusion(bf16[256,24]{1,0:T(8,128)(2,1)S(1)} %get-tuple-element.37, bf16[256,1792]{1,0:T(8,128)(2,1)S(1)} %add_convert_fusion, bf16[256,1536]{1,0:T(8,128)(2,1)S(1)} %copy-done.11, bf16[1,256,768]{2,1,0:T(8,128)(2,1)S(1)} %copy-done.7, f32[768]{0:T(1024)S(1)} %copy-done.27, f32[256]{0:T(256)S(1)} %copy-done.28), kind=kOutput, calls=%fused_computation | convolution fusion | flops 1326569472 | bytes 7262208 | tf_op jit(solution)/shard_map/dot_general | solution.py:16
  164.5 5.4 %fusion.12 = (f32[768]{0:T(1024)S(1)}, f32[256]{0:T(256)S(1)}, f32[256,768]{1,0:T(8,128)}) fusion(bf16[1,256,768]{2,1,0:T(8,128)(2,1)S(1)} %copy-done.8, f32[256]{0:T(256)S(1)} %copy-done.28, f32[768]{0:T(1024)S(1)} %copy-done.27, bf16[768,3352]{1,0:T(8,128)(2,1)} %all-gather.3.cloned.1.call-done, bf16[256,24]{1,0:T(8,128)(2,1)S(1)} %copy-done.35, ...), kind=kOutput, calls=%fused_computation.39 | convolution fusion | flops 1324583936 | bytes 8052736 | tf_op jit(solution)/shard_map/dot_general | solution.py:16
  170.0 39.2 %psum.7 = f32[11336]{0:T(1024)S(1)} all-reduce(f32[11336]{0:T(1024)S(1)} %concatenate.38), channel_id=1, replica_groups=mesh['dp'=16,'rep'=2] {'dp','rep'}, use_global_device_ids=true, to_apply=%region_15.16 | all-reduce | flops 11336 | bytes 90688 | tf_op jit(solution)/shard_map/psum | solution.py:276
  209.8 0.7 slice.111
  212.3 2.1 fusion.16
  214.4 3.3 fusion.3
  217.7 5.4 %all_gather.15 = bf16[96,768]{1,0:T(8,128)(2,1)S(1)} all-gather(bf16[48,768]{1,0:T(8,128)(2,1)} %reduce-scatter.5.cloned.1.call-done), channel_id=1, replica_groups=mesh['dp'=16,'rep'=2] {'rep'}, dimensions={0}, use_global_device_ids=true | all-gather | bytes 221184 | tf_op jit(solution)/shard_map/all_gather | solution.py:227
  223.1 0.7 convert_element_type.49
  223.8 100.4 %reduce-scatter.7.cloned.1.call-done = bf16[24,3352]{1,0:T(8,128)(2,1)} async-done(((bf16[768,3352]{1,0:T(8,128)(2,1)}), bf16[24,3352]{1,0:T(8,128)(2,1)}) %reduce-scatter.7.cloned.1.call-update) | async-done | bytes 160912
  324.3 6.2 %all_gather.14 = bf16[48,3352]{1,0:T(8,128)(2,1)S(1)} all-gather(bf16[24,3352]{1,0:T(8,128)(2,1)} %reduce-scatter.7.cloned.1.call-done), channel_id=1, replica_groups=mesh['dp'=16,'rep'=2] {'rep'}, dimensions={0}, use_global_device_ids=true | all-gather | bytes 482688 | tf_op jit(solution)/shard_map/all_gather | solution.py:227
  330.5 0.9 convert_element_type.47
  (100 shorter events, 6.8 us)
Async XLA Ops:
  7.2 62.1 %all-gather.3.cloned.1.call-start = ((), (), s32[]{:S(2)}) async-start(), calls=%async_computation.2 | async-start | bytes 5640192 | tf_op jit(solution)/shard_map/all_gather | solution.py:236
  7.9 104.5 %all-gather.5.cloned.1.call-start = ((), (), s32[]{:S(2)}) async-start(), calls=%async_computation.3 | async-start | bytes 2506752 | tf_op jit(solution)/shard_map/all_gather | solution.py:237
  8.7 209.0 %reduce-scatter.5.cloned.1.call-start = ((), (), s32[]{:S(2)}) async-start(), calls=%async_computation.4 | async-start | bytes 2433024 | tf_op jit(solution)/shard_map/reduce_scatter | solution.py:226
  12.2 1.2 copy-start.25
  73.6 14.8 %copy-start.1 = (f32[256,3352]{1,0:T(8,128)}, f32[256,3352]{1,0:T(8,128)S(1)}, u32[]{:S(2)}) copy-start(f32[256,3352]{1,0:T(8,128)S(1)} %fusion.27) | copy-start | bytes 10297348
  76.6 1.4 copy-start.29
  76.6 1.4 copy-start.33
  94.0 10.6 %copy-start = (f32[256,1792]{1,0:T(8,128)S(1)}, f32[256,1792]{1,0:T(8,128)}, u32[]{:S(2)}) copy-start(f32[256,1792]{1,0:T(8,128)} %get-tuple-element.41.values.b_ref.c_ref) | copy-start | bytes 5505028
  104.5 2.6 copy-start.5
  104.5 2.6 copy-start.12
  107.1 8.9 %copy-start.15 = (f32[256]{0:T(256)}, f32[256]{0:T(256)S(1)}, u32[]{:S(2)}) copy-start(f32[256]{0:T(256)S(1)} %add_rsqrt_fusion) | copy-start | bytes 3076
  109.5 214.7 %reduce-scatter.7.cloned.1.call-start = ((), (), s32[]{:S(2)}) async-start(), calls=%async_computation.5 | async-start | bytes 5474304
  112.5 3.5 %copy-start.3 = (f32[256,1536]{1,0:T(8,128)S(1)}, f32[256,1536]{1,0:T(8,128)}, u32[]{:S(2)}) copy-start(f32[256,1536]{1,0:T(8,128)} %scan_forward.1) | copy-start | bytes 4718596
  120.5 15.3 %copy-start.4 = (f32[256,1536]{1,0:T(8,128)S(1)}, f32[256,1536]{1,0:T(8,128)}, u32[]{:S(2)}) copy-start(f32[256,1536]{1,0:T(8,128)} %get-tuple-element.35.grad) | copy-start | bytes 4718596
  135.8 2.5 copy-start.2
  135.8 2.5 copy-start.13
  135.8 2.5 copy-start.14
  145.9 1.4 copy-start.24
  154.9 3.2 copy-start.34
  154.9 4.2 %copy-start.7 = (bf16[1,256,768]{2,1,0:T(8,128)(2,1)S(1)}, bf16[1,256,768]{2,1,0:T(8,128)(2,1)}, u32[]{:S(2)}) copy-start(bf16[1,256,768]{2,1,0:T(8,128)(2,1)} %param.11) | copy-start | bytes 1179652
  154.9 4.2 %copy-start.11 = (bf16[256,1536]{1,0:T(8,128)(2,1)S(1)}, bf16[256,1536]{1,0:T(8,128)(2,1)}, u32[]{:S(2)}) copy-start(bf16[256,1536]{1,0:T(8,128)(2,1)} %get-tuple-element.43) | copy-start | bytes 2359300
  154.9 4.2 %copy-start.27 = (f32[768]{0:T(1024)S(1)}, f32[768]{0:T(1024)}, u32[]{:S(2)}) copy-start(f32[768]{0:T(1024)} %param.12) | copy-start | bytes 9220
  154.9 4.2 %copy-start.28 = (f32[256]{0:T(256)S(1)}, f32[256]{0:T(256)}, u32[]{:S(2)}) copy-start(f32[256]{0:T(256)} %add_rsqrt_fusion.1) | copy-start | bytes 3076
  158.1 0.9 copy-start.9
  163.1 0.7 copy-start.18
  163.1 0.8 copy-start.23
  163.1 0.8 copy-start.22
  163.1 0.8 copy-start.21
  163.1 0.8 copy-start.20
  163.1 1.0 copy-start.31
  163.1 1.0 copy-start.32
  163.1 1.1 copy-start.8
  163.1 1.4 copy-start.10
  163.1 1.4 copy-start.35
  164.5 5.4 %copy-start.17 = (f32[1536]{0:T(1024)S(1)}, f32[1536]{0:T(1024)}, u32[]{:S(2)}) copy-start(f32[1536]{0:T(1024)} %get-tuple-element.21) | copy-start | bytes 18436
  164.5 5.4 %copy-start.19 = (f32[1792]{0:T(1024)S(1)}, f32[1792]{0:T(1024)}, u32[]{:S(2)}) copy-start(f32[1792]{0:T(1024)} %get-tuple-element.23) | copy-start | bytes 21508
  164.5 5.4 %copy-start.30 = (f32[24]{0:T(128)S(1)}, f32[24]{0:T(128)}, u32[]{:S(2)}) copy-start(f32[24]{0:T(128)} %get-tuple-element.36) | copy-start | bytes 292
  164.5 47.2 %copy-start.26 = (f32[256]{0:T(256)S(1)}, f32[256]{0:T(256)}, u32[]{:S(2)}) copy-start(f32[256]{0:T(256)} %copy-done.25) | copy-start | bytes 3076
  164.5 47.8 %copy-start.6 = (bf16[1,256,768]{2,1,0:T(8,128)(2,1)S(1)}, bf16[1,256,768]{2,1,0:T(8,128)(2,1)}, u32[]{:S(2)}) copy-start(bf16[1,256,768]{2,1,0:T(8,128)(2,1)} %param.21) | copy-start | bytes 1179652
  169.9 44.5 %copy-start.16 = (f32[256]{0:T(256)S(1)}, f32[256]{0:T(256)}, u32[]{:S(2)}) copy-start(f32[256]{0:T(256)} %copy-done.15) | copy-start | bytes 3076
Sparse Core Ops, SparseCore 0:
  10.2 59.0 all-gather.2
  71.5 40.8 all-gather.4
  117.7 98.2 reduce-scatter.4
  221.6 102.6 reduce-scatter.6
